TPU v7x, 256 devices: a whole 4x4x8 slice. The times are simulated.
256 devices in a mesh: seq: 32 (over x, y, core), head: 8 (over z).
Axes of the slice: x: 4, y: 4, z: 8, core: 2. Of those that a mesh axis runs over, the one named last changes fastest.
Arguments:
- projected: bfloat16 [49152, 6912], P(('seq', 'head')), may hold values from -10 to 10
- segment_ids: int32 [49152], replicated, may hold values from 0 to 63, never falling along the last dimension, each value on 1 to 1536 neighbouring positions
- widths: int32 [64], replicated, may hold values from 16 to 64
Outputs:
- attended: bfloat16 [49152, 2304], P(('seq', 'head'))
Inputs may be any that keep to these rules, and one draw needn't show every extreme that they name: `segment_ids`: ids never fall along the sequence; each of the 64 samples covers 1 to 1536 consecutive positions and some sample covers exactly 1536.
All inputs are finite; a program needn't handle non-finite values.
Results may differ from a plain program's by a relative error of at most 0.0088.
Values may be sent and summed in bfloat16 or wider, within the bound.
No kernel may reach another device: no remote copies, remote signals or barrier semaphores. Data moves between devices by JAX's collectives and lax.ppermute only.
A program may use at most 128 MiB of HBM per device.

v0:
```python
import math
import jax
import jax.numpy as jnp
from jax import lax
from jax.sharding import PartitionSpec as P

D = 2304
HEADS = 24
masked_score = -1e30


def with_halo(shard, sides, width):
    for axis, dim in sides:
        size, length = (lax.axis_size(axis), shard.shape[dim])
        up = [(i, (i + 1) % size) for i in range(size - 1)]
        down = [(j, i) for i, j in up]
        last = lax.slice_in_dim(shard, length - width, length, axis=dim)
        first = lax.slice_in_dim(shard, 0, width, axis=dim)
        before = lax.ppermute(last, axis, up)
        after = lax.ppermute(first, axis, down)
        shard = jnp.concatenate([before, shard, after], axis=dim)
    return shard


def shortened(shard):

    def short(part):
        return part.astype(jnp.bfloat16) if part.dtype == jnp.float32 else part

    return jax.tree.map(short, shard)


def rotate(head_vals, row_pos, col_pos):
    quarter = head_vals.shape[-1] // 4
    frequency = 10000.0 ** (-jnp.arange(quarter, dtype=jnp.float32) / quarter)

    def turn(half_vals, place):
        angles = place.astype(jnp.float32)[:, None] * frequency[None, :]
        cosine = jnp.cos(angles)[:, None, :]
        sine_part = jnp.sin(angles)[:, None, :]
        first_half = half_vals[..., :quarter]
        second = half_vals[..., quarter:]
        return jnp.concatenate(
            [first_half * cosine - second * sine_part, first_half * sine_part + second * cosine],
            axis=-1,
        )

    middle = 2 * quarter
    return jnp.concatenate(
        [turn(head_vals[..., :middle], row_pos), turn(head_vals[..., middle:], col_pos)], axis=-1
    )


def starts_of(segment_ids):
    length = segment_ids.shape[0]
    indices = jnp.arange(length, dtype=jnp.int32)
    before = jnp.concatenate([jnp.full((1,), -1, jnp.int32), segment_ids[:-1]])
    return lax.cummax(jnp.where(segment_ids != before, indices, 0), axis=0)


def block_scores(q_rows, k_rows, q_ids, k_ids, scaling):
    scores = (
        lax.dot_general(
            q_rows, k_rows, (((1,), (1,)), ((), ())), preferred_element_type=jnp.float32
        )
        * scaling
    )
    same_seg = q_ids[:, None] == k_ids[None, :]
    return (jnp.where(same_seg, scores, masked_score), same_seg)


def dense_rows(q_rows, k_all, v_all, q_ids, k_ids, scaling):
    scores, same_seg = block_scores(q_rows, k_all, q_ids, k_ids, scaling)
    row_max = jnp.max(scores, axis=1, keepdims=True)
    weights = jnp.where(same_seg, jnp.exp(scores - row_max), 0.0)
    totals = jnp.sum(weights, axis=1, keepdims=True)
    blended = jnp.dot(weights.astype(jnp.bfloat16), v_all, preferred_element_type=jnp.float32)
    return (blended / totals).astype(jnp.bfloat16)


def attend(queries, key_rows, values, query_seg, key_seg):
    shard_rows, head_count, head_size = queries.shape
    block_rows = min(512, shard_rows)
    scaling = 1.0 / math.sqrt(head_size)

    def one_block(number):
        start_row = number * block_rows
        q_blk = lax.dynamic_slice_in_dim(queries, start_row, block_rows, 0)
        q_ids = lax.dynamic_slice_in_dim(query_seg, start_row, block_rows, 0)
        outputs = []
        for head_num in range(head_count):
            outputs.append(
                dense_rows(
                    q_blk[:, head_num],
                    key_rows[:, head_num],
                    values[:, head_num],
                    q_ids,
                    key_seg,
                    scaling,
                )
            )
        return jnp.stack(outputs, axis=1)

    results = lax.map(one_block, jnp.arange(shard_rows // block_rows, dtype=jnp.int32))
    return results.reshape(shard_rows, head_count, head_size)


def body(projected, segment_ids, widths):
    tok_dev = projected.shape[0]
    group_size = lax.axis_size("head")
    shard_rows = tok_dev * group_size
    head_size = D // HEADS
    local_heads = HEADS // group_size
    seq_index = lax.axis_index("seq")
    head_index = lax.axis_index("head")
    first_tok = (seq_index * group_size + head_index) * tok_dev
    starts = starts_of(segment_ids)
    own_seg = lax.dynamic_slice_in_dim(segment_ids, first_tok, tok_dev, 0)
    own_start = lax.dynamic_slice_in_dim(starts, first_tok, tok_dev, 0)
    offset = first_tok + jnp.arange(tok_dev, dtype=jnp.int32) - own_start
    sample_ids = jnp.arange(widths.shape[0], dtype=jnp.int32)
    width_tok = jnp.sum(
        jnp.where(own_seg[:, None] == sample_ids[None, :], widths[None, :], 0), axis=1
    )
    row_pos = offset // width_tok
    col_pos = offset % width_tok
    qkv_parts = projected.reshape(tok_dev, 3, HEADS, head_size)
    q_rot = rotate(qkv_parts[:, 0].astype(jnp.float32), row_pos, col_pos).astype(jnp.bfloat16)
    k_rot = rotate(qkv_parts[:, 1].astype(jnp.float32), row_pos, col_pos).astype(jnp.bfloat16)
    stacked = jnp.stack([q_rot, k_rot, qkv_parts[:, 2]], axis=1)
    stacked = stacked.reshape(tok_dev, 3, group_size, local_heads, head_size)
    query_seg = lax.dynamic_slice_in_dim(segment_ids, seq_index * shard_rows, shard_rows, 0)
    no_sample = jnp.full((shard_rows,), -1, jnp.int32)
    seg_pad = jnp.concatenate([no_sample, segment_ids, no_sample], axis=0)
    key_seg = lax.dynamic_slice_in_dim(seg_pad, seq_index * shard_rows, 3 * shard_rows, 0)
    qkv_part = lax.all_to_all(stacked, "head", split_axis=2, concat_axis=0, tiled=True)
    key_value = qkv_part[:, 1:]
    widened = with_halo(key_value, (("seq", 0),), qkv_part.shape[0])
    attended_heads = attend(
        qkv_part[:, 0, 0], widened[:, 0, 0], widened[:, 1, 0], query_seg, key_seg
    )
    returned = lax.all_to_all(
        shortened(attended_heads), "head", split_axis=0, concat_axis=1, tiled=True
    ).astype(attended_heads.dtype)
    return returned.reshape(tok_dev, HEADS * head_size)


def solution(mesh):
    in_specs = (P(("seq", "head"), None), P(), P())
    out_specs = P(("seq", "head"), None)
    return jax.shard_map(body, mesh=mesh, in_specs=in_specs, out_specs=out_specs, check_vma=False)
```

profile of v0, /device:TPU:6, one launch (start us, length us, event | category | flops | bytes accessed | tf_op | source)
XLA Modules:
  0.0 286.2 jit_solution(3814066336356876828)
XLA Ops:
  3.8 4.8 %copy.34 = bf16[192,6912]{0,1:T(8,128)(2,1)S(1)} copy(bf16[192,6912]{1,0:T(8,128)(2,1)} %param.5) | data formatting | bytes 5308416 | tf_op args[0]
  12.1 90.4 %all_to_all.33 = bf16[192,3,8,3,96]{0,4,3,1,2:T(8,128)(2,1)S(1)} all-to-all(bf16[192,3,8,3,96]{0,4,3,1,2:T(8,128)(2,1)S(1)} %copy.39), channel_id=1, replica_groups=mesh['seq'=32,'head'=8] {'head'}, dimensions={2} | all-to-all | bytes 5308416 | tf_op jit(solution)/shard_map/all_to_all | solution.py:136
  102.5 2.2 copy.40
  104.7 4.1 %all_to_all.27 = bf16[1536,3,1,3,96]{0,4,3,1,2:T(8,128)(2,1)} reshape(bf16[8,192,3,1,3,96]{1,0,5,4,2,3:T(8,128)(2,1)S(1)} %copy.40) | data formatting | bytes 5308416 | tf_op jit(solution)/shard_map/all_to_all | solution.py:136
  110.4 1.9 collective-permute-start
  112.3 5.8 %collective-permute-start.1 = (bf16[1536,2,1,3,96]{0,4,3,1,2:T(8,128)(2,1)S(1)}, bf16[1536,2,1,3,96]{0,4,3,1,2:T(8,128)(2,1)}, u32[]{:S(2)}, u32[]{:S(2)}) collective-permute-start(bf16[1536,2,1,3,96]{0,4,3,1,2:T(8,128)(2,1)S(1)} %slice.133), channel_id=1, source_target_pairs={{8,0},{16,8},{24,16},{32,24},{40,32},{48,40},{56,48},{64,56},{72,6... | collective-permute-start | bytes 5308424 | tf_op jit(solution)/shard_map/ppermute | solution.py:20
  120.3 2.2 slice_bitcast_fusion.4
  122.5 13.8 %collective-permute-done = bf16[1536,2,1,3,96]{0,4,3,1,2:T(8,128)(2,1)S(1)} collective-permute-done((bf16[1536,2,1,3,96]{0,4,3,1,2:T(8,128)(2,1)S(1)}, bf16[1536,2,1,3,96]{0,4,3,1,2:T(8,128)(2,1)S(1)}, u32[]{:S(2)}, u32[]{:S(2)}) %collective-permute-start) | collective-permute-done | bytes 1769504 | tf_op jit(solution)/shard_map/ppermute | solution.py:19
  138.1 2.4 pad_maximum_fusion
  142.3 97.8 %while.10 = (s32[]{:T(128)}, bf16[3,512,3,96]{1,3,2,0:T(8,128)(2,1)S(1)}, s32[3]{0:T(128)S(1)}, s32[1536]{0:T(1024)S(1)}, s32[4608]{0:T(1024)}, /*index=5*/bf16[...) while((s32[]{:T(128)}, ...), condition=%wide.region_11.12_spmd, body=%wide.region_4.11_spmd.sunk | while | flops 2799301632 | bytes 157868512 | solution.py:104
  143.8 6.4 %fusion.89 = (f32[512]{0:T(512)S(1)}, f32[512,4608]{1,0:T(8,128)}) fusion(bf16[4608,3,96]{0,2,1:T(8,128)(2,1)} %get-tuple-element.199, bf16[1536,3,96]{0,2,1:T(8,128)(2,1)} %get-tuple-element.198, s32[]{:T(128)S(6)} %select_n.123, s32[]{:T(128)S(6)} %add.94, s32[4608]{0:T(1024)} %get-tuple-element.197, s32[512]{0:T(512)S(1)} %dynamic_slice.48), kind=kOutput, calls=%fused_computation.91.clone.1 | convolution fusion | flops 462421504 | bytes 10444808 | tf_op jit(solution)/shard_map/while/body/eval_jaxpr/dot_general | solution.py:63
  150.2 6.5 %fusion.88 = (f32[512]{0:T(512)S(1)}, f32[512,4608]{1,0:T(8,128)}) fusion(bf16[4608,3,96]{0,2,1:T(8,128)(2,1)} %get-tuple-element.199, bf16[1536,3,96]{0,2,1:T(8,128)(2,1)} %get-tuple-element.198, s32[]{:T(128)S(6)} %select_n.123, s32[4608]{0:T(1024)S(1)} %copy-done.2, s32[512]{0:T(512)S(1)} %dynamic_slice.48), kind=kOutput, calls=%fused_computation.90.clone.1 | convolution fusion | flops 462421504 | bytes 10442756 | tf_op jit(solution)/shard_map/while/body/eval_jaxpr/dot_general | solution.py:63
  156.8 3.0 %fusion.87 = (f32[512]{0:T(512)S(1)}, f32[512,4608]{1,0:T(8,128)S(1)}) fusion(bf16[4608,3,96]{0,2,1:T(8,128)(2,1)} %get-tuple-element.199, bf16[1536,3,96]{0,2,1:T(8,128)(2,1)} %get-tuple-element.198, s32[]{:T(128)S(6)} %select_n.123, s32[]{:T(128)S(6)} %add.93, s32[4608]{0:T(1024)} %get-tuple-element.197, s32[512]{0:T(512)S(1)} %dynamic_slice.48), kind=kOutput, calls=%fused_computation.89.clone.1 | convolution fusion | flops 462421504 | bytes 10444808 | tf_op jit(solution)/shard_map/while/body/eval_jaxpr/dot_general | solution.py:63
  160.8 8.5 %fusion.90 = (f32[512]{0:T(512)S(1)}, f32[512]{0:T(512)S(1)}, f32[512]{0:T(512)S(1)}) fusion(f32[512,4608]{1,0:T(8,128)S(1)} %copy-done, f32[512]{0:T(512)S(1)} %get-tuple-element.159, s32[4608]{0:T(1024)S(1)} %copy-done.3, s32[512]{0:T(512)S(1)} %dynamic_slice.48, f32[512,4608]{1,0:T(8,128)} %get-tuple-element.160, f32[512]{0:T(512)S(1)} %get-tuple-element.161, ...), kind=kLoop, calls=%fused_computation.6.clone.1 | loop fusion | flops 23591424 | bytes 28344320 | tf_op jit(solution)/shard_map/while/body/eval_jaxpr/reduce_sum | solution.py:76
  169.3 1.8 fusion.93
  171.2 1.8 fusion.92
  173.0 1.8 fusion.91
  176.4 6.5 %fusion.89 = (f32[512]{0:T(512)S(1)}, f32[512,4608]{1,0:T(8,128)}) fusion(bf16[4608,3,96]{0,2,1:T(8,128)(2,1)} %get-tuple-element.199, bf16[1536,3,96]{0,2,1:T(8,128)(2,1)} %get-tuple-element.198, s32[]{:T(128)S(6)} %select_n.123, s32[]{:T(128)S(6)} %add.94, s32[4608]{0:T(1024)} %get-tuple-element.197, s32[512]{0:T(512)S(1)} %dynamic_slice.48), kind=kOutput, calls=%fused_computation.91.clone.1 | convolution fusion | flops 462421504 | bytes 10444808 | tf_op jit(solution)/shard_map/while/body/eval_jaxpr/dot_general | solution.py:63
  182.9 6.5 %fusion.88 = (f32[512]{0:T(512)S(1)}, f32[512,4608]{1,0:T(8,128)}) fusion(bf16[4608,3,96]{0,2,1:T(8,128)(2,1)} %get-tuple-element.199, bf16[1536,3,96]{0,2,1:T(8,128)(2,1)} %get-tuple-element.198, s32[]{:T(128)S(6)} %select_n.123, s32[4608]{0:T(1024)S(1)} %copy-done.2, s32[512]{0:T(512)S(1)} %dynamic_slice.48), kind=kOutput, calls=%fused_computation.90.clone.1 | convolution fusion | flops 462421504 | bytes 10442756 | tf_op jit(solution)/shard_map/while/body/eval_jaxpr/dot_general | solution.py:63
  189.4 3.0 %fusion.87 = (f32[512]{0:T(512)S(1)}, f32[512,4608]{1,0:T(8,128)S(1)}) fusion(bf16[4608,3,96]{0,2,1:T(8,128)(2,1)} %get-tuple-element.199, bf16[1536,3,96]{0,2,1:T(8,128)(2,1)} %get-tuple-element.198, s32[]{:T(128)S(6)} %select_n.123, s32[]{:T(128)S(6)} %add.93, s32[4608]{0:T(1024)} %get-tuple-element.197, s32[512]{0:T(512)S(1)} %dynamic_slice.48), kind=kOutput, calls=%fused_computation.89.clone.1 | convolution fusion | flops 462421504 | bytes 10444808 | tf_op jit(solution)/shard_map/while/body/eval_jaxpr/dot_general | solution.py:63
  193.4 8.5 %fusion.90 = (f32[512]{0:T(512)S(1)}, f32[512]{0:T(512)S(1)}, f32[512]{0:T(512)S(1)}) fusion(f32[512,4608]{1,0:T(8,128)S(1)} %copy-done, f32[512]{0:T(512)S(1)} %get-tuple-element.159, s32[4608]{0:T(1024)S(1)} %copy-done.3, s32[512]{0:T(512)S(1)} %dynamic_slice.48, f32[512,4608]{1,0:T(8,128)} %get-tuple-element.160, f32[512]{0:T(512)S(1)} %get-tuple-element.161, ...), kind=kLoop, calls=%fused_computation.6.clone.1 | loop fusion | flops 23591424 | bytes 28344320 | tf_op jit(solution)/shard_map/while/body/eval_jaxpr/reduce_sum | solution.py:76
  201.9 1.8 fusion.93
  203.8 1.8 fusion.92
  205.7 1.8 fusion.91
  209.0 6.5 %fusion.89 = (f32[512]{0:T(512)S(1)}, f32[512,4608]{1,0:T(8,128)}) fusion(bf16[4608,3,96]{0,2,1:T(8,128)(2,1)} %get-tuple-element.199, bf16[1536,3,96]{0,2,1:T(8,128)(2,1)} %get-tuple-element.198, s32[]{:T(128)S(6)} %select_n.123, s32[]{:T(128)S(6)} %add.94, s32[4608]{0:T(1024)} %get-tuple-element.197, s32[512]{0:T(512)S(1)} %dynamic_slice.48), kind=kOutput, calls=%fused_computation.91.clone.1 | convolution fusion | flops 462421504 | bytes 10444808 | tf_op jit(solution)/shard_map/while/body/eval_jaxpr/dot_general | solution.py:63
  215.5 6.5 %fusion.88 = (f32[512]{0:T(512)S(1)}, f32[512,4608]{1,0:T(8,128)}) fusion(bf16[4608,3,96]{0,2,1:T(8,128)(2,1)} %get-tuple-element.199, bf16[1536,3,96]{0,2,1:T(8,128)(2,1)} %get-tuple-element.198, s32[]{:T(128)S(6)} %select_n.123, s32[4608]{0:T(1024)S(1)} %copy-done.2, s32[512]{0:T(512)S(1)} %dynamic_slice.48), kind=kOutput, calls=%fused_computation.90.clone.1 | convolution fusion | flops 462421504 | bytes 10442756 | tf_op jit(solution)/shard_map/while/body/eval_jaxpr/dot_general | solution.py:63
  222.0 3.0 %fusion.87 = (f32[512]{0:T(512)S(1)}, f32[512,4608]{1,0:T(8,128)S(1)}) fusion(bf16[4608,3,96]{0,2,1:T(8,128)(2,1)} %get-tuple-element.199, bf16[1536,3,96]{0,2,1:T(8,128)(2,1)} %get-tuple-element.198, s32[]{:T(128)S(6)} %select_n.123, s32[]{:T(128)S(6)} %add.93, s32[4608]{0:T(1024)} %get-tuple-element.197, s32[512]{0:T(512)S(1)} %dynamic_slice.48), kind=kOutput, calls=%fused_computation.89.clone.1 | convolution fusion | flops 462421504 | bytes 10444808 | tf_op jit(solution)/shard_map/while/body/eval_jaxpr/dot_general | solution.py:63
  226.0 8.5 %fusion.90 = (f32[512]{0:T(512)S(1)}, f32[512]{0:T(512)S(1)}, f32[512]{0:T(512)S(1)}) fusion(f32[512,4608]{1,0:T(8,128)S(1)} %copy-done, f32[512]{0:T(512)S(1)} %get-tuple-element.159, s32[4608]{0:T(1024)S(1)} %copy-done.3, s32[512]{0:T(512)S(1)} %dynamic_slice.48, f32[512,4608]{1,0:T(8,128)} %get-tuple-element.160, f32[512]{0:T(512)S(1)} %get-tuple-element.161, ...), kind=kLoop, calls=%fused_computation.6.clone.1 | loop fusion | flops 23591424 | bytes 28344320 | tf_op jit(solution)/shard_map/while/body/eval_jaxpr/reduce_sum | solution.py:76
  234.5 1.8 fusion.93
  236.4 1.8 fusion.92
  238.3 1.8 fusion.91
  241.2 42.7 %all_to_all.34 = bf16[1536,3,96]{2,1,0:T(4,128)(2,1)S(1)} all-to-all(bf16[1536,3,96]{2,1,0:T(4,128)(2,1)S(1)} %bitcast.128), channel_id=1, replica_groups=mesh['seq'=32,'head'=8] {'head'}, dimensions={0} | all-to-all | bytes 1769472 | tf_op jit(solution)/shard_map/all_to_all | solution.py:142
  (97 shorter events, 23.2 us)
Async XLA Ops:
  3.8 5.3 %copy-start.6 = (s32[64]{0:T(128)S(1)}, s32[64]{0:T(128)}, u32[]{:S(2)}) copy-start(s32[64]{0:T(128)} %param.7) | copy-start | bytes 772
  110.4 26.0 %collective-permute-start = (bf16[1536,2,1,3,96]{0,4,3,1,2:T(8,128)(2,1)S(1)}, bf16[1536,2,1,3,96]{0,4,3,1,2:T(8,128)(2,1)S(1)}, u32[]{:S(2)}, u32[]{:S(2)}) collective-permute-start(bf16[1536,2,1,3,96]{0,4,3,1,2:T(8,128)(2,1)S(1)} %slice.133), channel_id=1, source_target_pairs={{0,8},{8,16},{16,24},{24,32},{32,40},{40,48},{48,56},{56,64},{64,7... | collective-permute-start | bytes 5308424 | tf_op jit(solution)/shard_map/ppermute | solution.py:19
  112.3 25.8 %collective-permute-start.1 = (bf16[1536,2,1,3,96]{0,4,3,1,2:T(8,128)(2,1)S(1)}, bf16[1536,2,1,3,96]{0,4,3,1,2:T(8,128)(2,1)}, u32[]{:S(2)}, u32[]{:S(2)}) collective-permute-start(bf16[1536,2,1,3,96]{0,4,3,1,2:T(8,128)(2,1)S(1)} %slice.133), channel_id=1, source_target_pairs={{8,0},{16,8},{24,16},{32,24},{40,32},{48,40},{56,48},{64,56},{72,6... | collective-permute-start | bytes 5308424 | tf_op jit(solution)/shard_map/ppermute | solution.py:20
  140.5 1.8 copy-start.1
  142.3 1.4 copy-start.4
  143.8 6.5 %copy-start.2 = (s32[4608]{0:T(1024)S(1)}, s32[4608]{0:T(1024)}, u32[]{:S(2)}) copy-start(s32[4608]{0:T(1024)} %get-tuple-element.197) | copy-start | bytes 55300 | tf_op jit(solution)/shard_map/while
  156.8 4.0 %copy-start = (f32[512,4608]{1,0:T(8,128)S(1)}, f32[512,4608]{1,0:T(8,128)}, u32[]{:S(2)}) copy-start(f32[512,4608]{1,0:T(8,128)} %get-tuple-element.158) | copy-start | bytes 28311556 | tf_op jit(solution)/shard_map/while
  156.8 4.0 %copy-start.3 = (s32[4608]{0:T(1024)S(1)}, s32[4608]{0:T(1024)}, u32[]{:S(2)}) copy-start(s32[4608]{0:T(1024)} %get-tuple-element.197) | copy-start | bytes 55300 | tf_op jit(solution)/shard_map/while
  160.8 10.4 %slice-start = ((s8[9437184]{0:T(1024)(128)(4,1)}), s8[4194304]{0:T(1024)(128)(4,1)S(1)}, s32[]{:S(2)}) async-start(s8[9437184]{0:T(1024)(128)(4,1)} %bitcast.124), calls=%async_computation.2 | async-start | bytes 8388608 | tf_op jit(solution)/shard_map/while
  160.8 10.4 %slice-start.1 = ((s8[9437184]{0:T(1024)(128)(4,1)}), s8[4194304]{0:T(1024)(128)(4,1)S(1)}, s32[]{:S(2)}) async-start(s8[9437184]{0:T(1024)(128)(4,1)} %bitcast.124), calls=%async_computation.3 | async-start | bytes 8388608 | tf_op jit(solution)/shard_map/while
  169.3 1.9 slice-start.2
  173.0 1.9 copy-start.5
  174.9 1.5 copy-start.4
  176.4 6.5 %copy-start.2 = (s32[4608]{0:T(1024)S(1)}, s32[4608]{0:T(1024)}, u32[]{:S(2)}) copy-start(s32[4608]{0:T(1024)} %get-tuple-element.197) | copy-start | bytes 55300 | tf_op jit(solution)/shard_map/while
  189.4 4.0 %copy-start = (f32[512,4608]{1,0:T(8,128)S(1)}, f32[512,4608]{1,0:T(8,128)}, u32[]{:S(2)}) copy-start(f32[512,4608]{1,0:T(8,128)} %get-tuple-element.158) | copy-start | bytes 28311556 | tf_op jit(solution)/shard_map/while
  189.4 4.0 %copy-start.3 = (s32[4608]{0:T(1024)S(1)}, s32[4608]{0:T(1024)}, u32[]{:S(2)}) copy-start(s32[4608]{0:T(1024)} %get-tuple-element.197) | copy-start | bytes 55300 | tf_op jit(solution)/shard_map/while
  193.4 10.4 %slice-start = ((s8[9437184]{0:T(1024)(128)(4,1)}), s8[4194304]{0:T(1024)(128)(4,1)S(1)}, s32[]{:S(2)}) async-start(s8[9437184]{0:T(1024)(128)(4,1)} %bitcast.124), calls=%async_computation.2 | async-start | bytes 8388608 | tf_op jit(solution)/shard_map/while
  193.4 10.4 %slice-start.1 = ((s8[9437184]{0:T(1024)(128)(4,1)}), s8[4194304]{0:T(1024)(128)(4,1)S(1)}, s32[]{:S(2)}) async-start(s8[9437184]{0:T(1024)(128)(4,1)} %bitcast.124), calls=%async_computation.3 | async-start | bytes 8388608 | tf_op jit(solution)/shard_map/while
  201.9 1.9 slice-start.2
  205.6 1.9 copy-start.5
  207.6 1.5 copy-start.4
  209.0 6.5 %copy-start.2 = (s32[4608]{0:T(1024)S(1)}, s32[4608]{0:T(1024)}, u32[]{:S(2)}) copy-start(s32[4608]{0:T(1024)} %get-tuple-element.197) | copy-start | bytes 55300 | tf_op jit(solution)/shard_map/while
  222.0 4.0 %copy-start = (f32[512,4608]{1,0:T(8,128)S(1)}, f32[512,4608]{1,0:T(8,128)}, u32[]{:S(2)}) copy-start(f32[512,4608]{1,0:T(8,128)} %get-tuple-element.158) | copy-start | bytes 28311556 | tf_op jit(solution)/shard_map/while
  222.0 4.0 %copy-start.3 = (s32[4608]{0:T(1024)S(1)}, s32[4608]{0:T(1024)}, u32[]{:S(2)}) copy-start(s32[4608]{0:T(1024)} %get-tuple-element.197) | copy-start | bytes 55300 | tf_op jit(solution)/shard_map/while
  226.0 10.4 %slice-start = ((s8[9437184]{0:T(1024)(128)(4,1)}), s8[4194304]{0:T(1024)(128)(4,1)S(1)}, s32[]{:S(2)}) async-start(s8[9437184]{0:T(1024)(128)(4,1)} %bitcast.124), calls=%async_computation.2 | async-start | bytes 8388608 | tf_op jit(solution)/shard_map/while
  226.0 10.4 %slice-start.1 = ((s8[9437184]{0:T(1024)(128)(4,1)}), s8[4194304]{0:T(1024)(128)(4,1)S(1)}, s32[]{:S(2)}) async-start(s8[9437184]{0:T(1024)(128)(4,1)} %bitcast.124), calls=%async_computation.3 | async-start | bytes 8388608 | tf_op jit(solution)/shard_map/while
  234.5 1.9 slice-start.2
  238.3 1.9 copy-start.5
where the time goes:
time: 287 us; the launch traced here: 286 us
  blocking collectives  133 us (46%)
  matrix products  64.6 us (23%)
  other arithmetic  34.4 us (12%)
  local copies, waits for them, and re-layouts  28.2 us (10%)
  waiting for transfers between devices  15.6 us (5%)
  starting transfers between devices  7.67 us (3%)
    all_to_all x1, blocking collectives, body(): lax.all_to_all(stacked, 'head', split_axis=2, concat_axis=0, tiled=True)  90.4 us
    dot_general x9, matrix products, block_scores(): lax.dot_general(q_rows, k_rows, (((1,), (1,)), ((), ())), preferred_eleme...  48.1 us
    all_to_all x1, blocking collectives, body(): lax.all_to_all(shortened(attended_heads), 'head', split_axis=0, concat_ax...  42.7 us
    reduce_sum x3, other arithmetic, dense_rows(): totals = jnp.sum(weights, axis=1, keepdims=True)  25.5 us
    dot_general x9, matrix products, dense_rows(): jnp.dot(weights.astype(jnp.bfloat16), v_all, preferred_element_type=jnp.f...  16.5 us
    ppermute x1, waiting for transfers between devices, with_halo(): before = lax.ppermute(last, axis, up)  13.8 us
    all_to_all x2, local copies, waits for them, and re-layouts, body(): lax.all_to_all(stacked, 'head', split_axis=2, concat_axis=0, tiled=True)  6.32 us
    ppermute x1, starting transfers between devices, with_halo(): after = lax.ppermute(first, axis, down)  5.75 us
  transfers between devices with their start and end apart: 2, of which 2 were waited for; matrix products, arithmetic and copies ran while one was open for 2% of the time, Pallas kernels for 0%

commit v1 on v0

--- a/solution.py
+++ b/solution.py
@@ -7,6 +7,13 @@
 D = 2304
 HEADS = 24
 masked_score = -1e30
+
+
+def swap_blocks(array, axis, split, join):
+    size = lax.axis_size(axis)
+    blocks = jnp.stack(jnp.split(array, size, axis=split), axis=0)
+    blocks = lax.all_to_all(blocks, axis, split_axis=0, concat_axis=0)
+    return jnp.concatenate(blocks, axis=join)
 
 
 def with_halo(shard, sides, width):
@@ -139,9 +146,7 @@
     attended_heads = attend(
         qkv_part[:, 0, 0], widened[:, 0, 0], widened[:, 1, 0], query_seg, key_seg
     )
-    returned = lax.all_to_all(
-        shortened(attended_heads), "head", split_axis=0, concat_axis=1, tiled=True
-    ).astype(attended_heads.dtype)
+    returned = swap_blocks(shortened(attended_heads), "head", 0, 1).astype(attended_heads.dtype)
     return returned.reshape(tok_dev, HEADS * head_size)
 
 

time: 287 us -> 276 us (0.962)
  blocking collectives: 133 us -> 125 us
    all_to_all x1, blocking collectives: 42.7 us -> 34.2 us  [swap_blocks(): blocks = lax.all_to_all(blocks, axis, split_axis=0, concat_axis=0)]
where the time goes in v1:
time: 276 us; the launch traced here: 275 us
  blocking collectives  125 us (45%)
  matrix products  64.6 us (23%)
  other arithmetic  33.4 us (12%)
  local copies, waits for them, and re-layouts  26.9 us (10%)
  waiting for transfers between devices  15.6 us (6%)
  starting transfers between devices  7.67 us (3%)
    all_to_all x1, blocking collectives, body(): lax.all_to_all(stacked, 'head', split_axis=2, concat_axis=0, tiled=True)  90.4 us
    dot_general x9, matrix products, block_scores(): lax.dot_general(q_rows, k_rows, (((1,), (1,)), ((), ())), preferred_eleme...  48.1 us
    all_to_all x1, blocking collectives, swap_blocks(): blocks = lax.all_to_all(blocks, axis, split_axis=0, concat_axis=0)  34.2 us
    reduce_sum x3, other arithmetic, dense_rows(): totals = jnp.sum(weights, axis=1, keepdims=True)  24.5 us
    dot_general x9, matrix products, dense_rows(): jnp.dot(weights.astype(jnp.bfloat16), v_all, preferred_element_type=jnp.f...  16.5 us
    ppermute x1, waiting for transfers between devices, with_halo(): before = lax.ppermute(last, axis, up)  13.8 us
    all_to_all x2, local copies, waits for them, and re-layouts, body(): lax.all_to_all(stacked, 'head', split_axis=2, concat_axis=0, tiled=True)  6.32 us
    ppermute x1, starting transfers between devices, with_halo(): after = lax.ppermute(first, axis, down)  5.75 us
  transfers between devices with their start and end apart: 2, of which 2 were waited for; matrix products, arithmetic and copies ran while one was open for 2% of the time, Pallas kernels for 0%

profile of v1, /device:TPU:6, one launch (start us, length us, event | category | flops | bytes accessed | tf_op | source)
XLA Modules:
  0.0 275.4 jit_solution(11196415709342648191)
XLA Ops:
  3.8 4.8 %copy.36 = bf16[192,6912]{0,1:T(8,128)(2,1)S(1)} copy(bf16[192,6912]{1,0:T(8,128)(2,1)} %param.5) | data formatting | bytes 5308416 | tf_op args[0]
  12.2 90.4 %all_to_all.23 = bf16[192,3,8,3,96]{0,4,3,1,2:T(8,128)(2,1)S(1)} all-to-all(bf16[192,3,8,3,96]{0,4,3,1,2:T(8,128)(2,1)S(1)} %copy.41), channel_id=1, replica_groups=mesh['seq'=32,'head'=8] {'head'}, dimensions={2} | all-to-all | bytes 5308416 | tf_op jit(solution)/shard_map/all_to_all | solution.py:143
  102.6 2.2 copy.42
  104.8 4.1 %all_to_all.19 = bf16[1536,3,1,3,96]{0,4,3,1,2:T(8,128)(2,1)} reshape(bf16[8,192,3,1,3,96]{1,0,5,4,2,3:T(8,128)(2,1)S(1)} %copy.42) | data formatting | bytes 5308416 | tf_op jit(solution)/shard_map/all_to_all | solution.py:143
  110.5 1.9 collective-permute-start
  112.4 5.8 %collective-permute-start.1 = (bf16[1536,2,1,3,96]{0,4,3,1,2:T(8,128)(2,1)S(1)}, bf16[1536,2,1,3,96]{0,4,3,1,2:T(8,128)(2,1)}, u32[]{:S(2)}, u32[]{:S(2)}) collective-permute-start(bf16[1536,2,1,3,96]{0,4,3,1,2:T(8,128)(2,1)S(1)} %slice.133), channel_id=1, source_target_pairs={{8,0},{16,8},{24,16},{32,24},{40,32},{48,40},{56,48},{64,56},{72,6... | collective-permute-start | bytes 5308424 | tf_op jit(solution)/shard_map/ppermute | solution.py:27
  120.4 2.2 slice_bitcast_fusion.4
  122.6 13.8 %collective-permute-done = bf16[1536,2,1,3,96]{0,4,3,1,2:T(8,128)(2,1)S(1)} collective-permute-done((bf16[1536,2,1,3,96]{0,4,3,1,2:T(8,128)(2,1)S(1)}, bf16[1536,2,1,3,96]{0,4,3,1,2:T(8,128)(2,1)S(1)}, u32[]{:S(2)}, u32[]{:S(2)}) %collective-permute-start) | collective-permute-done | bytes 1769504 | tf_op jit(solution)/shard_map/ppermute | solution.py:26
  138.2 2.4 pad_maximum_fusion
  142.5 96.8 %while.10 = (s32[]{:T(128)}, bf16[3,512,3,96]{1,3,2,0:T(8,128)(2,1)S(1)}, s32[3]{0:T(128)S(1)}, s32[1536]{0:T(1024)S(1)}, s32[4608]{0:T(1024)}, /*index=5*/bf16[...) while((s32[]{:T(128)}, ...), condition=%wide.region_11.12_spmd, body=%wide.region_4.11_spmd.sunk | while | flops 2799301632 | bytes 157868512 | solution.py:111
  143.9 6.5 %fusion.97 = (f32[512]{0:T(512)S(1)}, f32[512,4608]{1,0:T(8,128)}) fusion(bf16[4608,3,96]{0,2,1:T(8,128)(2,1)} %get-tuple-element.199, bf16[1536,3,96]{0,2,1:T(8,128)(2,1)} %get-tuple-element.198, s32[]{:T(128)S(6)} %select_n.123, s32[]{:T(128)S(6)} %add.94, s32[4608]{0:T(1024)} %get-tuple-element.197, s32[512]{0:T(512)S(1)} %dynamic_slice.48), kind=kOutput, calls=%fused_computation.107.clone.1 | convolution fusion | flops 462421504 | bytes 10444808 | tf_op jit(solution)/shard_map/while/body/eval_jaxpr/dot_general | solution.py:70
  150.4 6.5 %fusion.96 = (f32[512]{0:T(512)S(1)}, f32[512,4608]{1,0:T(8,128)}) fusion(bf16[4608,3,96]{0,2,1:T(8,128)(2,1)} %get-tuple-element.199, bf16[1536,3,96]{0,2,1:T(8,128)(2,1)} %get-tuple-element.198, s32[]{:T(128)S(6)} %select_n.123, s32[4608]{0:T(1024)S(1)} %copy-done.2, s32[512]{0:T(512)S(1)} %dynamic_slice.48), kind=kOutput, calls=%fused_computation.106.clone.1 | convolution fusion | flops 462421504 | bytes 10442756 | tf_op jit(solution)/shard_map/while/body/eval_jaxpr/dot_general | solution.py:70
  156.9 3.0 %fusion.95 = (f32[512]{0:T(512)S(1)}, f32[512,4608]{1,0:T(8,128)S(1)}) fusion(bf16[4608,3,96]{0,2,1:T(8,128)(2,1)} %get-tuple-element.199, bf16[1536,3,96]{0,2,1:T(8,128)(2,1)} %get-tuple-element.198, s32[]{:T(128)S(6)} %select_n.123, s32[]{:T(128)S(6)} %add.93, s32[4608]{0:T(1024)} %get-tuple-element.197, s32[512]{0:T(512)S(1)} %dynamic_slice.48), kind=kOutput, calls=%fused_computation.105.clone.1 | convolution fusion | flops 462421504 | bytes 10444808 | tf_op jit(solution)/shard_map/while/body/eval_jaxpr/dot_general | solution.py:70
  160.9 8.2 %fusion.98 = (f32[512]{0:T(512)S(1)}, f32[512]{0:T(512)S(1)}, f32[512]{0:T(512)S(1)}) fusion(f32[512,4608]{1,0:T(8,128)} %get-tuple-element.158, f32[512]{0:T(512)S(1)} %get-tuple-element.159, s32[4608]{0:T(1024)} %get-tuple-element.197, s32[512]{0:T(512)S(1)} %dynamic_slice.48, f32[512,4608]{1,0:T(8,128)S(1)} %copy-done, ...), kind=kLoop, calls=%fused_computation.6.clone.1 | loop fusion | flops 23591424 | bytes 28344320 | tf_op jit(solution)/shard_map/while/body/eval_jaxpr/reduce_sum | solution.py:83
  169.1 1.8 fusion.101
  171.0 1.8 fusion.100
  172.8 1.8 fusion.99
  176.2 6.5 %fusion.97 = (f32[512]{0:T(512)S(1)}, f32[512,4608]{1,0:T(8,128)}) fusion(bf16[4608,3,96]{0,2,1:T(8,128)(2,1)} %get-tuple-element.199, bf16[1536,3,96]{0,2,1:T(8,128)(2,1)} %get-tuple-element.198, s32[]{:T(128)S(6)} %select_n.123, s32[]{:T(128)S(6)} %add.94, s32[4608]{0:T(1024)} %get-tuple-element.197, s32[512]{0:T(512)S(1)} %dynamic_slice.48), kind=kOutput, calls=%fused_computation.107.clone.1 | convolution fusion | flops 462421504 | bytes 10444808 | tf_op jit(solution)/shard_map/while/body/eval_jaxpr/dot_general | solution.py:70
  182.7 6.5 %fusion.96 = (f32[512]{0:T(512)S(1)}, f32[512,4608]{1,0:T(8,128)}) fusion(bf16[4608,3,96]{0,2,1:T(8,128)(2,1)} %get-tuple-element.199, bf16[1536,3,96]{0,2,1:T(8,128)(2,1)} %get-tuple-element.198, s32[]{:T(128)S(6)} %select_n.123, s32[4608]{0:T(1024)S(1)} %copy-done.2, s32[512]{0:T(512)S(1)} %dynamic_slice.48), kind=kOutput, calls=%fused_computation.106.clone.1 | convolution fusion | flops 462421504 | bytes 10442756 | tf_op jit(solution)/shard_map/while/body/eval_jaxpr/dot_general | solution.py:70
  189.2 3.0 %fusion.95 = (f32[512]{0:T(512)S(1)}, f32[512,4608]{1,0:T(8,128)S(1)}) fusion(bf16[4608,3,96]{0,2,1:T(8,128)(2,1)} %get-tuple-element.199, bf16[1536,3,96]{0,2,1:T(8,128)(2,1)} %get-tuple-element.198, s32[]{:T(128)S(6)} %select_n.123, s32[]{:T(128)S(6)} %add.93, s32[4608]{0:T(1024)} %get-tuple-element.197, s32[512]{0:T(512)S(1)} %dynamic_slice.48), kind=kOutput, calls=%fused_computation.105.clone.1 | convolution fusion | flops 462421504 | bytes 10444808 | tf_op jit(solution)/shard_map/while/body/eval_jaxpr/dot_general | solution.py:70
  193.2 8.2 %fusion.98 = (f32[512]{0:T(512)S(1)}, f32[512]{0:T(512)S(1)}, f32[512]{0:T(512)S(1)}) fusion(f32[512,4608]{1,0:T(8,128)} %get-tuple-element.158, f32[512]{0:T(512)S(1)} %get-tuple-element.159, s32[4608]{0:T(1024)} %get-tuple-element.197, s32[512]{0:T(512)S(1)} %dynamic_slice.48, f32[512,4608]{1,0:T(8,128)S(1)} %copy-done, ...), kind=kLoop, calls=%fused_computation.6.clone.1 | loop fusion | flops 23591424 | bytes 28344320 | tf_op jit(solution)/shard_map/while/body/eval_jaxpr/reduce_sum | solution.py:83
  201.4 1.8 fusion.101
  203.2 1.8 fusion.100
  205.1 1.8 fusion.99
  208.4 6.5 %fusion.97 = (f32[512]{0:T(512)S(1)}, f32[512,4608]{1,0:T(8,128)}) fusion(bf16[4608,3,96]{0,2,1:T(8,128)(2,1)} %get-tuple-element.199, bf16[1536,3,96]{0,2,1:T(8,128)(2,1)} %get-tuple-element.198, s32[]{:T(128)S(6)} %select_n.123, s32[]{:T(128)S(6)} %add.94, s32[4608]{0:T(1024)} %get-tuple-element.197, s32[512]{0:T(512)S(1)} %dynamic_slice.48), kind=kOutput, calls=%fused_computation.107.clone.1 | convolution fusion | flops 462421504 | bytes 10444808 | tf_op jit(solution)/shard_map/while/body/eval_jaxpr/dot_general | solution.py:70
  214.9 6.5 %fusion.96 = (f32[512]{0:T(512)S(1)}, f32[512,4608]{1,0:T(8,128)}) fusion(bf16[4608,3,96]{0,2,1:T(8,128)(2,1)} %get-tuple-element.199, bf16[1536,3,96]{0,2,1:T(8,128)(2,1)} %get-tuple-element.198, s32[]{:T(128)S(6)} %select_n.123, s32[4608]{0:T(1024)S(1)} %copy-done.2, s32[512]{0:T(512)S(1)} %dynamic_slice.48), kind=kOutput, calls=%fused_computation.106.clone.1 | convolution fusion | flops 462421504 | bytes 10442756 | tf_op jit(solution)/shard_map/while/body/eval_jaxpr/dot_general | solution.py:70
  221.4 3.0 %fusion.95 = (f32[512]{0:T(512)S(1)}, f32[512,4608]{1,0:T(8,128)S(1)}) fusion(bf16[4608,3,96]{0,2,1:T(8,128)(2,1)} %get-tuple-element.199, bf16[1536,3,96]{0,2,1:T(8,128)(2,1)} %get-tuple-element.198, s32[]{:T(128)S(6)} %select_n.123, s32[]{:T(128)S(6)} %add.93, s32[4608]{0:T(1024)} %get-tuple-element.197, s32[512]{0:T(512)S(1)} %dynamic_slice.48), kind=kOutput, calls=%fused_computation.105.clone.1 | convolution fusion | flops 462421504 | bytes 10444808 | tf_op jit(solution)/shard_map/while/body/eval_jaxpr/dot_general | solution.py:70
  225.4 8.2 %fusion.98 = (f32[512]{0:T(512)S(1)}, f32[512]{0:T(512)S(1)}, f32[512]{0:T(512)S(1)}) fusion(f32[512,4608]{1,0:T(8,128)} %get-tuple-element.158, f32[512]{0:T(512)S(1)} %get-tuple-element.159, s32[4608]{0:T(1024)} %get-tuple-element.197, s32[512]{0:T(512)S(1)} %dynamic_slice.48, f32[512,4608]{1,0:T(8,128)S(1)} %copy-done, ...), kind=kLoop, calls=%fused_computation.6.clone.1 | loop fusion | flops 23591424 | bytes 28344320 | tf_op jit(solution)/shard_map/while/body/eval_jaxpr/reduce_sum | solution.py:83
  233.7 1.8 fusion.101
  235.5 1.8 fusion.100
  237.4 1.8 fusion.99
  239.9 34.2 %all_to_all.24 = bf16[8,192,3,96]{1,3,2,0:T(8,128)(2,1)S(1)} all-to-all(bf16[8,192,3,96]{1,3,2,0:T(8,128)(2,1)S(1)} %fusion.60), channel_id=1, replica_groups=mesh['seq'=32,'head'=8] {'head'}, dimensions={0} | all-to-all | bytes 1769472 | tf_op jit(solution)/shard_map/all_to_all | solution.py:15
  (104 shorter events, 21.9 us)
Async XLA Ops:
  8.6 0.7 copy-start.6
  110.5 26.0 %collective-permute-start = (bf16[1536,2,1,3,96]{0,4,3,1,2:T(8,128)(2,1)S(1)}, bf16[1536,2,1,3,96]{0,4,3,1,2:T(8,128)(2,1)S(1)}, u32[]{:S(2)}, u32[]{:S(2)}) collective-permute-start(bf16[1536,2,1,3,96]{0,4,3,1,2:T(8,128)(2,1)S(1)} %slice.133), channel_id=1, source_target_pairs={{0,8},{8,16},{16,24},{24,32},{32,40},{40,48},{48,56},{56,64},{64,7... | collective-permute-start | bytes 5308424 | tf_op jit(solution)/shard_map/ppermute | solution.py:26
  112.4 25.8 %collective-permute-start.1 = (bf16[1536,2,1,3,96]{0,4,3,1,2:T(8,128)(2,1)S(1)}, bf16[1536,2,1,3,96]{0,4,3,1,2:T(8,128)(2,1)}, u32[]{:S(2)}, u32[]{:S(2)}) collective-permute-start(bf16[1536,2,1,3,96]{0,4,3,1,2:T(8,128)(2,1)S(1)} %slice.133), channel_id=1, source_target_pairs={{8,0},{16,8},{24,16},{32,24},{40,32},{48,40},{56,48},{64,56},{72,6... | collective-permute-start | bytes 5308424 | tf_op jit(solution)/shard_map/ppermute | solution.py:27
  140.6 1.8 copy-start.1
  142.5 1.4 copy-start.4
  143.9 6.5 %copy-start.2 = (s32[4608]{0:T(1024)S(1)}, s32[4608]{0:T(1024)}, u32[]{:S(2)}) copy-start(s32[4608]{0:T(1024)} %get-tuple-element.197) | copy-start | bytes 55300 | tf_op jit(solution)/shard_map/while
  156.9 4.0 %copy-start = (f32[512,4608]{1,0:T(8,128)S(1)}, f32[512,4608]{1,0:T(8,128)}, u32[]{:S(2)}) copy-start(f32[512,4608]{1,0:T(8,128)} %get-tuple-element.160) | copy-start | bytes 28311556 | tf_op jit(solution)/shard_map/while
  156.9 12.2 %slice-start = ((s8[9437184]{0:T(1024)(128)(4,1)}), s8[4194304]{0:T(1024)(128)(4,1)S(1)}, s32[]{:S(2)}) async-start(s8[9437184]{0:T(1024)(128)(4,1)} %bitcast.155), calls=%async_computation.2 | async-start | bytes 8388608 | tf_op jit(solution)/shard_map/while
  160.9 8.2 %slice-start.1 = ((s8[9437184]{0:T(1024)(128)(4,1)}), s8[4194304]{0:T(1024)(128)(4,1)S(1)}, s32[]{:S(2)}) async-start(s8[9437184]{0:T(1024)(128)(4,1)} %bitcast.155), calls=%async_computation.3 | async-start | bytes 8388608 | tf_op jit(solution)/shard_map/while
  160.9 8.2 %slice-start.2 = ((s8[9437184]{0:T(1024)(128)(4,1)}), s8[1048576]{0:T(1024)(128)(4,1)S(1)}, s32[]{:S(2)}) async-start(s8[9437184]{0:T(1024)(128)(4,1)} %bitcast.155), calls=%async_computation.4 | async-start | bytes 2097152 | tf_op jit(solution)/shard_map/while
  160.9 8.2 %copy-start.3 = (s32[4608]{0:T(1024)S(1)}, s32[4608]{0:T(1024)}, u32[]{:S(2)}) copy-start(s32[4608]{0:T(1024)} %get-tuple-element.197) | copy-start | bytes 55300 | tf_op jit(solution)/shard_map/while
  172.8 1.9 copy-start.5
  174.7 1.5 copy-start.4
  176.2 6.5 %copy-start.2 = (s32[4608]{0:T(1024)S(1)}, s32[4608]{0:T(1024)}, u32[]{:S(2)}) copy-start(s32[4608]{0:T(1024)} %get-tuple-element.197) | copy-start | bytes 55300 | tf_op jit(solution)/shard_map/while
  189.2 4.0 %copy-start = (f32[512,4608]{1,0:T(8,128)S(1)}, f32[512,4608]{1,0:T(8,128)}, u32[]{:S(2)}) copy-start(f32[512,4608]{1,0:T(8,128)} %get-tuple-element.160) | copy-start | bytes 28311556 | tf_op jit(solution)/shard_map/while
  189.2 12.2 %slice-start = ((s8[9437184]{0:T(1024)(128)(4,1)}), s8[4194304]{0:T(1024)(128)(4,1)S(1)}, s32[]{:S(2)}) async-start(s8[9437184]{0:T(1024)(128)(4,1)} %bitcast.155), calls=%async_computation.2 | async-start | bytes 8388608 | tf_op jit(solution)/shard_map/while
  193.2 8.2 %slice-start.1 = ((s8[9437184]{0:T(1024)(128)(4,1)}), s8[4194304]{0:T(1024)(128)(4,1)S(1)}, s32[]{:S(2)}) async-start(s8[9437184]{0:T(1024)(128)(4,1)} %bitcast.155), calls=%async_computation.3 | async-start | bytes 8388608 | tf_op jit(solution)/shard_map/while
  193.2 8.2 %slice-start.2 = ((s8[9437184]{0:T(1024)(128)(4,1)}), s8[1048576]{0:T(1024)(128)(4,1)S(1)}, s32[]{:S(2)}) async-start(s8[9437184]{0:T(1024)(128)(4,1)} %bitcast.155), calls=%async_computation.4 | async-start | bytes 2097152 | tf_op jit(solution)/shard_map/while
  193.2 8.2 %copy-start.3 = (s32[4608]{0:T(1024)S(1)}, s32[4608]{0:T(1024)}, u32[]{:S(2)}) copy-start(s32[4608]{0:T(1024)} %get-tuple-element.197) | copy-start | bytes 55300 | tf_op jit(solution)/shard_map/while
  205.1 1.9 copy-start.5
  207.0 1.5 copy-start.4
  208.4 6.5 %copy-start.2 = (s32[4608]{0:T(1024)S(1)}, s32[4608]{0:T(1024)}, u32[]{:S(2)}) copy-start(s32[4608]{0:T(1024)} %get-tuple-element.197) | copy-start | bytes 55300 | tf_op jit(solution)/shard_map/while
  221.4 4.0 %copy-start = (f32[512,4608]{1,0:T(8,128)S(1)}, f32[512,4608]{1,0:T(8,128)}, u32[]{:S(2)}) copy-start(f32[512,4608]{1,0:T(8,128)} %get-tuple-element.160) | copy-start | bytes 28311556 | tf_op jit(solution)/shard_map/while
  221.4 12.2 %slice-start = ((s8[9437184]{0:T(1024)(128)(4,1)}), s8[4194304]{0:T(1024)(128)(4,1)S(1)}, s32[]{:S(2)}) async-start(s8[9437184]{0:T(1024)(128)(4,1)} %bitcast.155), calls=%async_computation.2 | async-start | bytes 8388608 | tf_op jit(solution)/shard_map/while
  225.4 8.2 %slice-start.1 = ((s8[9437184]{0:T(1024)(128)(4,1)}), s8[4194304]{0:T(1024)(128)(4,1)S(1)}, s32[]{:S(2)}) async-start(s8[9437184]{0:T(1024)(128)(4,1)} %bitcast.155), calls=%async_computation.3 | async-start | bytes 8388608 | tf_op jit(solution)/shard_map/while
  225.4 8.2 %slice-start.2 = ((s8[9437184]{0:T(1024)(128)(4,1)}), s8[1048576]{0:T(1024)(128)(4,1)S(1)}, s32[]{:S(2)}) async-start(s8[9437184]{0:T(1024)(128)(4,1)} %bitcast.155), calls=%async_computation.4 | async-start | bytes 2097152 | tf_op jit(solution)/shard_map/while
  225.4 8.2 %copy-start.3 = (s32[4608]{0:T(1024)S(1)}, s32[4608]{0:T(1024)}, u32[]{:S(2)}) copy-start(s32[4608]{0:T(1024)} %get-tuple-element.197) | copy-start | bytes 55300 | tf_op jit(solution)/shard_map/while
  237.3 1.9 copy-start.5
